TPU v7x, 128 devices: a whole 4x4x4 slice. The times are simulated.
128 devices in a mesh: seq: 8 (over x, core), tensor: 8 (over z, y_lo), dp: 2 (over y_hi).
Axes of the slice: x: 4, y: 4 (y_hi: 2, y_lo: 2; y = y_hi * 2 + y_lo), z: 4, core: 2. Of those that a mesh axis runs over, the one named last changes fastest.
Arguments:
- ssm_input: bfloat16 [2, 2048, 8192], P('dp', 'seq', 'tensor'), may hold values from -6 to 6
- b_input: bfloat16 [2, 2048, 1024], P('dp', 'seq', 'tensor'), may hold values from -0.125 to 0.125
- c_input: bfloat16 [2, 2048, 1024], P('dp', 'seq', 'tensor'), may hold values from -0.125 to 0.125
- step_size: float32 [2, 128, 2048], P('dp', 'tensor', 'seq'), may hold values from 0 to 2048, as said below
- decay_rate: float32 [128], P('tensor'), may hold values from 0 to 1, as said below
- skip_gain: float32 [128], P('tensor'), may hold values from 0.5 to 2
- resets: int32 [2, 8], P('dp', 'seq'), may hold values 0 or 1
- out_grad: bfloat16 [2, 2048, 4096], P('dp', 'seq'), may hold values from -6 to 6
- out_weight: bfloat16 [4096, 8192], P(('seq', 'dp'), 'tensor'), may hold values from -0.0625 to 0.0625
Outputs:
- grad_input: bfloat16 [2, 2048, 8192], P('dp', 'seq', 'tensor')
- grad_b: float32 [2, 2048, 1024], P('dp', 'seq', 'tensor')
- grad_c: float32 [2, 2048, 1024], P('dp', 'seq', 'tensor')
- grad_weight: float32 [4096, 8192], P(('seq', 'dp'), 'tensor')
Inputs may be any that keep to these rules, and one draw needn't show every extreme that they name: `step_size`: positive per-position steps. `decay_rate`: positive per-head rates.
All inputs are finite; a program needn't handle non-finite values. No bound on the sum of `resets` on one device may be relied on, other than what follows from the above.
Results may differ from a plain program's by a relative error of at most 0.017.
Values may be sent and summed in bfloat16 or wider, within the bound.
A program may use at most 128 MiB of HBM per device.

v0:
```python
import jax
import jax.numpy as jnp
from jax import lax
from jax.sharding import PartitionSpec as P

P_SIZE = 64
N = 128
Q = 256


def prefix(value, axis, join, neutral, backward):
    count, mine = (lax.axis_size(axis), lax.axis_index(axis))
    pieces = jax.tree.map(lambda part: lax.all_gather(part, axis), value)
    if backward:
        pieces = jax.tree.map(lambda part: part[::-1], pieces)
        mine = count - 1 - mine
    running = jax.tree.map(
        lambda part, zero: jnp.full_like(part, 0) + jnp.asarray(zero, part.dtype), value, neutral
    )

    def step(position, running):
        longer = join(running, jax.tree.map(lambda part: part[position], pieces))
        return jax.tree.map(lambda new, old: jnp.where(position < mine, new, old), longer, running)

    return lax.fori_loop(0, count - 1, step, running)


def contract(pattern, former, latter):
    return jnp.einsum(pattern, former, latter, preferred_element_type=jnp.float32)


def block_tables(step_rows, head_rates):
    log_decay = jnp.cumsum(-step_rows * head_rates[..., None], axis=-1)
    last_log = log_decay[..., -1:]
    damping = jnp.exp(last_log[..., 0])
    to_end = jnp.moveaxis(jnp.exp(last_log - log_decay), -1, 0)[..., None]
    from_start = jnp.moveaxis(jnp.exp(log_decay), -1, 0)[..., None]
    positions = jnp.arange(log_decay.shape[-1])
    causal = positions[:, None] >= positions[None, :]
    spread = log_decay[..., :, None] - log_decay[..., None, :]
    weights = jnp.where(causal, jnp.exp(jnp.minimum(spread, 0.0)), 0.0)
    return (damping, to_end, from_start, weights)


def block_sums(inputs, b_rows, c_rows, grad_rows, to_end, from_start):
    weighted_in = (inputs.astype(jnp.float32) * to_end).astype(jnp.bfloat16)
    weighted_grad = (grad_rows.astype(jnp.float32) * from_start).astype(jnp.bfloat16)
    carried = contract("qgkp,qgn->gkpn", weighted_in, b_rows)
    adjoint = contract("qgkp,qgn->gkpn", weighted_grad, c_rows)
    return (carried, adjoint, weighted_in, weighted_grad)


def block_grads(
    inputs,
    b_rows,
    c_rows,
    grad_rows,
    skip_rows,
    to_end,
    from_start,
    weights,
    weighted_in,
    weighted_grad,
    state_in,
    adjoint_out,
):
    scores = contract("ign,jgn->gij", c_rows, b_rows)
    mixing = (weights * scores[:, None]).astype(jnp.bfloat16)
    skip_term = skip_rows[None, :, :, None]
    output = (
        contract("gkij,jgkp->igkp", mixing, inputs)
        + from_start * contract("gkpn,ign->igkp", state_in, c_rows)
        + skip_term * inputs.astype(jnp.float32)
    )
    grad_in = (
        contract("gkij,igkp->jgkp", mixing, grad_rows)
        + to_end * contract("gkpn,jgn->jgkp", adjoint_out, b_rows)
        + skip_term * grad_rows.astype(jnp.float32)
    )
    products = contract("igkp,jgkp->gkij", grad_rows, inputs)
    paired = (weights * products).astype(jnp.bfloat16)
    grad_b = contract("gkij,ign->jgn", paired, c_rows) + contract(
        "jgkp,gkpn->jgn", weighted_in, adjoint_out
    )
    grad_c = contract("gkij,jgn->ign", paired, b_rows) + contract(
        "igkp,gkpn->ign", weighted_grad, state_in
    )
    return (output.astype(jnp.bfloat16), grad_in.astype(jnp.bfloat16), grad_b, grad_c)


def forward_step(running, sliced):
    kept, carried, damping = sliced
    state_in = kept * running
    return (damping[..., None, None] * state_in + carried, state_in)


def backward_step(running, sliced):
    kept, adjoint, damping = sliced
    return (kept * (damping[..., None, None] * running + adjoint), running)


def compose(earlier, following):
    return (earlier[0] * following[0], following[0][..., None, None] * earlier[1] + following[1])


def body(
    ssm_input, b_input, c_input, step_size, decay_rate, skip_gain, resets, out_grad, out_weight
):
    head_count = decay_rate.shape[0]
    length = ssm_input.shape[1]
    blocks = length // Q
    incoming = out_grad[0]
    columns = incoming
    head_total = jnp.dot(
        columns,
        lax.all_gather(out_weight, ("seq", "dp"), axis=0, tiled=True),
        preferred_element_type=jnp.float32,
    )
    head_grad = head_total.astype(jnp.bfloat16)
    inputs = ssm_input[0].reshape(blocks, Q, 1, head_count, P_SIZE)
    b_rows = b_input[0].reshape(blocks, Q, 1, N)
    c_rows = c_input[0].reshape(blocks, Q, 1, N)
    grad_rows = head_grad.reshape(blocks, Q, 1, head_count, P_SIZE)
    step_rows = step_size[0].reshape(1, head_count, blocks, Q).transpose(2, 0, 1, 3)
    head_rates = decay_rate.reshape(1, head_count)
    skip_rows = skip_gain.reshape(1, head_count)
    keep_rows = (1 - resets[0]).astype(jnp.float32)
    decays, to_end, from_start, weights = jax.vmap(block_tables, in_axes=(0, None))(
        step_rows, head_rates
    )
    carried, adjoint, weighted_in, weighted_grad = jax.vmap(block_sums)(
        inputs, b_rows, c_rows, grad_rows, to_end, from_start
    )
    zero_state = jnp.zeros((1, head_count, P_SIZE, N), jnp.float32)
    local_out, local_states = lax.scan(forward_step, zero_state, (keep_rows, carried, decays))
    local_back, local_adjoints = lax.scan(
        backward_step, zero_state, (keep_rows, adjoint, decays), reverse=True
    )
    factors = keep_rows[:, None, None] * decays
    through = jnp.prod(factors, axis=0)
    unit_gain = jnp.ones_like(through)
    through_before, state_before = prefix(
        (through, local_out), "seq", compose, (unit_gain, zero_state), False
    )
    through_after, adjoint_after = prefix(
        (through, local_back), "seq", compose, (unit_gain, zero_state), True
    )
    final_state, states = lax.scan(forward_step, state_before, (keep_rows, carried, decays))
    final_adjoint, adjoints = lax.scan(
        backward_step, adjoint_after, (keep_rows, adjoint, decays), reverse=True
    )
    output, grad_in, grad_b, grad_c = jax.vmap(
        block_grads, in_axes=(0, 0, 0, 0, None, 0, 0, 0, 0, 0, 0, 0)
    )(
        inputs,
        b_rows,
        c_rows,
        grad_rows,
        skip_rows,
        to_end,
        from_start,
        weights,
        weighted_in,
        weighted_grad,
        states.astype(jnp.bfloat16),
        adjoints.astype(jnp.bfloat16),
    )
    outputs = output.reshape(length, head_count * P_SIZE)
    columns = incoming
    grad_weight = lax.psum_scatter(
        jnp.einsum("ld,lh->dh", columns, outputs, preferred_element_type=jnp.float32).astype(
            jnp.bfloat16
        ),
        ("seq", "dp"),
        scatter_dimension=0,
        tiled=True,
    ).astype(jnp.float32)
    return (
        grad_in.reshape(1, length, head_count * P_SIZE),
        grad_b.reshape(1, length, N),
        grad_c.reshape(1, length, N),
        grad_weight,
    )


def solution(mesh):
    in_specs = (
        P("dp", "seq", "tensor"),
        P("dp", "seq", "tensor"),
        P("dp", "seq", "tensor"),
        P("dp", "tensor", "seq"),
        P("tensor"),
        P("tensor"),
        P("dp", "seq"),
        P("dp", "seq", None),
        P(("seq", "dp"), "tensor"),
    )
    out_specs = (
        P("dp", "seq", "tensor"),
        P("dp", "seq", "tensor"),
        P("dp", "seq", "tensor"),
        P(("seq", "dp"), "tensor"),
    )
    return jax.shard_map(body, mesh=mesh, in_specs=in_specs, out_specs=out_specs, check_vma=False)
```

profile of v0, /device:TPU:1, one launch (start us, length us, event | category | flops | bytes accessed | tf_op | source)
XLA Modules:
  0.0 289.9 jit_solution(8070474870886657349)
XLA Ops:
  11.7 1.3 copy.106
  13.9 1.9 convolution_add_fusion
  18.0 12.0 %all-gather = f32[8,1,16,1]{2,3,1,0:T(1,128)S(1)} all-gather(f32[1,1,16,1]{2,3,1,0:T(1,128)} %get-tuple-element.390), channel_id=2, replica_groups=mesh['seq'=8,'tensor'=8,'dp'=2] {'seq'}, dimensions={0}, use_global_device_ids=true | all-gather | bytes 576 | tf_op jit(solution)/shard_map/all_gather | solution.py:13
  31.7 20.0 %all-gather.11.cloned.1.call-done = f32[128,64,128]{2,1,0:T(8,128)} async-done(((f32[16,64,128]{2,1,0:T(8,128)}), f32[128,64,128]{2,1,0:T(8,128)}) %all-gather.11.cloned.1.call-update) | async-done | bytes 4194320 | tf_op jit(solution)/shard_map/all_gather | solution.py:13
  51.7 8.5 %while.19 = (s32[]{:T(128)}, f32[1,16,64,128]{3,2,1,0:T(8,128)S(1)}, s32[]{:T(128)}, f32[8,1,16]{2,1,0:T(1,128)S(1)}, f32[8,1,16,64,128]{4,3,2,1,0:T(8,128)}, /*index=5*/s32[]{:T(128)}, s32[]{:T(128)}) while((s32[]{:T(128)}, f32[1,16,64,128]{3,2,1,0:T(8,128)S(1)}, s32[]{:T(128)}, f32[8,1,16]{2,1,0:T(1,128)S(1)}, ...), condition=%wide.region_6.7_spmd.clone, body=%wide.region_5.6_spmd.clone.sunk | while | flops 524292 | bytes 1573161 | solution.py:25
  51.7 1.2 fusion.61
  52.9 1.2 fusion.61
  54.1 1.2 fusion.61
  55.3 1.2 fusion.61
  56.5 1.2 fusion.61
  57.8 1.2 fusion.61
  59.0 1.2 fusion.61
  60.5 2.5 fusion.21
  63.0 5.7 %convert_bitcast_fusion = bf16[4096,1024]{0,1:T(8,128)(2,1)} fusion(bf16[256,1024]{0,1:T(8,128)(2,1)S(1)} %bitcast.203, bf16[1,256,4096]{2,1,0:T(8,128)(2,1)S(1)} %copy-done), kind=kOutput, calls=%fused_computation.6 | convolution fusion | flops 2151677952 | bytes 11010048 | tf_op jit(solution)/shard_map/ld,lh->dh/dot_general | solution.py:171
  70.0 2.6 copy.101
  72.6 54.2 %all-gather.7.cloned.1.call-done = bf16[4096,1024]{1,0:T(8,128)(2,1)} async-done(((bf16[256,1024]{1,0:T(8,128)(2,1)}), bf16[4096,1024]{1,0:T(8,128)(2,1)}) %all-gather.7.cloned.1.call-update) | async-done | bytes 8388624 | tf_op jit(solution)/shard_map/all_gather | solution.py:116
  126.8 7.0 %multiply_convert_fusion.20 = (bf16[256,1024]{1,0:T(8,128)(2,1)}, bf16[256,1024]{1,0:T(8,128)(2,1)}) fusion(f32[256,1024]{1,0:T(8,128)} %copy.101, bf16[4096,1024]{1,0:T(8,128)(2,1)} %all-gather.7.cloned.1.call-done, bf16[1,256,4096]{2,1,0:T(8,128)(2,1)S(1)} %copy-done), kind=kOutput, calls=%fused_computation.44 | convolution fusion | flops 2148532224 | bytes 12582912 | tf_op jit(solution)/shard_map/dot_general | solution.py:114
  133.8 1.2 copy.102
  136.3 2.2 copy.93
  138.5 2.3 copy.105
  140.7 1.5 convolution_bitcast_fusion.2
  142.2 2.8 convert_reduce_fusion
  145.8 84.1 %reduce-scatter.2.cloned.1.call-done = bf16[256,1024]{0,1:T(8,128)(2,1)} async-done(((bf16[4096,1024]{0,1:T(8,128)(2,1)}), bf16[256,1024]{0,1:T(8,128)(2,1)}) %reduce-scatter.2.cloned.1.call-update) | async-done | bytes 524304 | tf_op jit(solution)/shard_map/reduce_scatter | solution.py:170
  230.0 2.2 copy.113
  232.2 32.5 %all-gather.9.cloned.1.call-done = f32[128,64,128]{2,1,0:T(8,128)} async-done(((f32[16,64,128]{2,1,0:T(8,128)}), f32[128,64,128]{2,1,0:T(8,128)}) %all-gather.9.cloned.1.call-update) | async-done | bytes 4194320 | tf_op jit(solution)/shard_map/all_gather | solution.py:13
  264.6 4.9 %rev.7 = f32[8,1,16,64,128]{4,3,2,1,0:T(8,128)} reverse(f32[8,1,16,64,128]{4,3,2,1,0:T(8,128)} %bitcast.191), dimensions={0} | reverse | bytes 8388608 | tf_op jit(solution)/shard_map/rev | solution.py:15
  269.5 8.5 %while.18 = (s32[]{:T(128)}, f32[1,16,64,128]{3,2,1,0:T(8,128)S(1)}, s32[]{:T(128)}, f32[8,1,16]{2,1,0:T(1,128)S(1)}, f32[8,1,16,64,128]{4,3,2,1,0:T(8,128)}, /*index=5*/s32[]{:T(128)}, s32[]{:T(128)}) while((s32[]{:T(128)}, f32[1,16,64,128]{3,2,1,0:T(8,128)S(1)}, s32[]{:T(128)}, f32[8,1,16]{2,1,0:T(1,128)S(1)}, ...), condition=%wide.region_3.4_spmd.clone, body=%wide.region_2.3_spmd.clone.sunk | while | flops 524292 | bytes 1573161 | solution.py:25
  269.5 1.2 fusion.60
  272.0 1.2 fusion.60
  273.2 1.2 fusion.60
  274.4 1.2 fusion.60
  278.7 2.8 fusion.20
  (82 shorter events, 18.3 us)
Async XLA Ops:
  7.2 55.8 %copy-start = (bf16[1,256,4096]{2,1,0:T(8,128)(2,1)S(1)}, bf16[1,256,4096]{2,1,0:T(8,128)(2,1)}, u32[]{:S(2)}) copy-start(bf16[1,256,4096]{2,1,0:T(8,128)(2,1)} %param.20) | copy-start | bytes 6291460
  7.2 23.6 %copy-start.5 = (bf16[1,256,128]{2,1,0:T(8,128)(2,1)S(1)}, bf16[1,256,128]{2,1,0:T(8,128)(2,1)}, u32[]{:S(2)}) copy-start(bf16[1,256,128]{2,1,0:T(8,128)(2,1)} %param.14) | copy-start | bytes 196612
  7.2 23.6 %copy-start.6 = (bf16[1,256,128]{2,1,0:T(8,128)(2,1)S(1)}, bf16[1,256,128]{2,1,0:T(8,128)(2,1)}, u32[]{:S(2)}) copy-start(bf16[1,256,128]{2,1,0:T(8,128)(2,1)} %param.15) | copy-start | bytes 196612
  7.2 44.5 %all-gather.11.cloned.1.call-start = ((), (), s32[]{:S(2)}) async-start(), calls=%async_computation.4 | async-start | bytes 4718592 | tf_op jit(solution)/shard_map/all_gather | solution.py:13
  12.9 47.6 %copy-start.4 = (bf16[1,256,1024]{1,2,0:T(8,128)(2,1)}, bf16[1,256,1024]{1,2,0:T(8,128)(2,1)S(1)}, u32[]{:S(2)}) copy-start(bf16[1,256,1024]{1,2,0:T(8,128)(2,1)S(1)} %copy.106) | copy-start | bytes 1572868
  13.0 0.8 copy-start.2
  15.8 111.0 %all-gather.7.cloned.1.call-start = ((), (), s32[]{:S(2)}) async-start(), calls=%async_computation.1 | async-start | bytes 8912896 | tf_op jit(solution)/shard_map/all_gather | solution.py:116
  16.6 213.4 %reduce-scatter.2.cloned.1.call-start = ((), (), s32[]{:S(2)}) async-start(), calls=%async_computation.2 | async-start | bytes 8912896 | tf_op jit(solution)/shard_map/reduce_scatter | solution.py:170
  30.0 112.2 %copy-start.8 = (pred[256,256]{1,0:T(8,128)(4,1)}, pred[256,256]{1,0:T(8,128)(4,1)S(1)}, u32[]{:S(2)}) copy-start(pred[256,256]{1,0:T(8,128)(4,1)S(1)} %iota_compare_fusion) | copy-start | bytes 196612
  30.8 111.4 %copy-start.9 = (f32[16,256]{1,0:T(8,128)}, f32[16,256]{1,0:T(8,128)S(1)}, u32[]{:S(2)}) copy-start(f32[16,256]{1,0:T(8,128)S(1)} %bitcast_add_fusion.2) | copy-start | bytes 49156
  30.8 29.4 %copy-start.7 = (f32[256,16]{0,1:T(8,128)S(1)}, f32[256,16]{0,1:T(8,128)}, u32[]{:S(2)}) copy-start(f32[256,16]{0,1:T(8,128)} %copy.100) | copy-start | bytes 49156
  51.7 8.8 %copy-start.11 = (f32[16]{0:T(128)S(1)}, f32[16]{0:T(128)}, u32[]{:S(2)}) copy-start(f32[16]{0:T(128)} %param.18) | copy-start | bytes 196
  68.7 195.9 %all-gather.9.cloned.1.call-start = ((), (), s32[]{:S(2)}) async-start(), calls=%async_computation.3 | async-start | bytes 4718592 | tf_op jit(solution)/shard_map/all_gather | solution.py:13
  72.6 62.5 %copy-start.10 = (f32[16]{0:T(128)S(1)}, f32[16]{0:T(128)}, u32[]{:S(2)}) copy-start(f32[16]{0:T(128)} %get-tuple-element.389) | copy-start | bytes 196
  135.1 1.1 copy-start.1
  269.5 8.8 %copy-start.3 = (bf16[1,256,1024]{1,2,0:T(8,128)(2,1)S(1)}, bf16[1,256,1024]{1,2,0:T(8,128)(2,1)}, u32[]{:S(2)}) copy-start(bf16[1,256,1024]{1,2,0:T(8,128)(2,1)} %copy-done.2) | copy-start | bytes 1572868
Sparse Core Ops, SparseCore 0:
  15.9 35.6 all-gather.10
  54.1 72.6 all-gather.6
  131.2 98.7 reduce-scatter.1
  232.1 32.4 all-gather.8
where the time goes:
time: 291 us; the launch traced here: 290 us
  waiting for transfers between devices  192 us (66%)
  matrix products  28.8 us (10%)
  local copies, waits for them, and re-layouts  21.4 us (7%)
  other arithmetic  20.7 us (7%)
  between operations  14.7 us (5%)
  blocking collectives  12 us (4%)
    reduce_scatter x1, waiting for transfers between devices, body(): lax.psum_scatter(jnp.einsum('ld,lh->dh', columns, outputs, preferred_elem...  84.1 us
    all_gather x1, waiting for transfers between devices, body(): lax.all_gather(out_weight, ('seq', 'dp'), axis=0, tiled=True)  54.2 us
    all_gather x2, waiting for transfers between devices, prefix(): pieces = jax.tree.map(lambda part: lax.all_gather(part, axis), value)  52.5 us
    select_n x14, other arithmetic, step(): jnp.where(position < mine, new, old)  16.5 us
    dot_general x12, matrix products, contract(): jnp.einsum(pattern, former, latter, preferred_element_type=jnp.float32)  16.1 us
    all_gather x1, blocking collectives, prefix(): pieces = jax.tree.map(lambda part: lax.all_gather(part, axis), value)  12 us
    dot_general x1, matrix products, body(): jnp.dot(columns, lax.all_gather(out_weight, ('seq', 'dp'), axis=0, tiled=...  7.02 us
  transfers between devices with their start and end apart: 4, of which 4 were waited for; matrix products, arithmetic and copies ran while one was open for 15% of the time, Pallas kernels for 0%

commit v1 on v0

--- a/solution.py
+++ b/solution.py
@@ -113,7 +113,15 @@
     columns = incoming
     head_total = jnp.dot(
         columns,
-        lax.all_gather(out_weight, ("seq", "dp"), axis=0, tiled=True),
+        jnp.concatenate(
+            lax.all_to_all(
+                jnp.stack([out_weight for _ in range(lax.psum(1, ("seq", "dp")))]),
+                ("seq", "dp"),
+                0,
+                0,
+            ),
+            axis=0,
+        ),
         preferred_element_type=jnp.float32,
     )
     head_grad = head_total.astype(jnp.bfloat16)

time: 291 us -> 331 us (1.14)
  waiting for transfers between devices: 192 us -> 219 us
  starting transfers between devices: 0.34 us -> 8.7 us
  blocking collectives: 12 us -> 17.3 us
    all_to_all x0 -> x1, waiting for transfers between devices: none -> 136 us  [body(): lax.all_to_all(jnp.stack([out_weight for _ in range(lax.psum(1, ('seq', '...]
    all_gather x1 -> x0, waiting for transfers between devices: 54.2 us -> none  [body(): lax.all_gather(out_weight, ('seq', 'dp'), axis=0, tiled=True)]
    all_gather x2, waiting for transfers between devices: 52.5 us -> 0.01 us  [prefix(): pieces = jax.tree.map(lambda part: lax.all_gather(part, axis), value)]
    all_to_all x0 -> x1, starting transfers between devices: none -> 8.58 us  [body(): lax.all_to_all(jnp.stack([out_weight for _ in range(lax.psum(1, ('seq', '...]
    all_gather x1, blocking collectives: 12 us -> 17.3 us  [prefix(): pieces = jax.tree.map(lambda part: lax.all_gather(part, axis), value)]
    another operation x6 -> x7, local copies, waits for them, and re-layouts: 0.8 us -> 5.69 us  [the longest x1 5.5 us: body(): jnp.stack([out_weight for _ in range(lax.psum(1, ('seq', 'dp')))])]
  transfers between devices with their start and end apart: 4 -> 4, of which waited for: 4 -> 2; matrix products, arithmetic and copies ran while one was open for 15% -> 18% of each run, Pallas kernels for 0% -> 0%
where the time goes in v1:
time: 331 us; the launch traced here: 329 us
  waiting for transfers between devices  219 us (66%)
  matrix products  28.5 us (9%)
  local copies, waits for them, and re-layouts  23.1 us (7%)
  other arithmetic  17.5 us (5%)
  blocking collectives  17.3 us (5%)
  between operations  14.7 us (4%)
  starting transfers between devices  8.7 us (3%)
    all_to_all x1, waiting for transfers between devices, body(): lax.all_to_all(jnp.stack([out_weight for _ in range(lax.psum(1, ('seq', '...  136 us
    reduce_scatter x1, waiting for transfers between devices, body(): lax.psum_scatter(jnp.einsum('ld,lh->dh', columns, outputs, preferred_elem...  82.3 us
    all_gather x1, blocking collectives, prefix(): pieces = jax.tree.map(lambda part: lax.all_gather(part, axis), value)  17.3 us
    select_n x14, other arithmetic, step(): jnp.where(position < mine, new, old)  16.6 us
    dot_general x12, matrix products, contract(): jnp.einsum(pattern, former, latter, preferred_element_type=jnp.float32)  16.1 us
    all_to_all x1, starting transfers between devices, body(): lax.all_to_all(jnp.stack([out_weight for _ in range(lax.psum(1, ('seq', '...  8.58 us
    dot_general x1, matrix products, body(): jnp.dot(columns, jnp.concatenate(lax.all_to_all(jnp.stack([out_weight for...  6.8 us
  transfers between devices with their start and end apart: 4, of which 2 were waited for; matrix products, arithmetic and copies ran while one was open for 18% of the time, Pallas kernels for 0%

profile of v1, /device:TPU:1, one launch (start us, length us, event | category | flops | bytes accessed | tf_op | source)
XLA Modules:
  0.0 328.8 jit_solution(1407228045901389352)
XLA Ops:
  7.2 5.5 %stack.2 = bf16[16,256,1024]{2,1,0:T(8,128)(2,1)} broadcast(bf16[256,1024]{1,0:T(8,128)(2,1)} %param.21), dimensions={1,2} | broadcast | bytes 8912896 | tf_op jit(solution)/shard_map/stack | solution.py:118
  12.7 8.6 %all-to-all-start = ((bf16[16,256,1024]{2,1,0:T(8,128)(2,1)}), bf16[16,256,1024]{2,1,0:T(8,128)(2,1)}, u32[]{:S(2)}, u32[]{:S(2)}) async-start(bf16[16,256,1024]{2,1,0:T(8,128)(2,1)} %stack.2), calls=%async_computation | async-start | bytes 16777216 | tf_op jit(solution)/shard_map/all_to_all | solution.py:117
  23.2 1.3 copy.106
  26.7 1.3 copy.101
  28.0 136.3 %all-to-all-done = bf16[16,256,1024]{2,1,0:T(8,128)(2,1)} async-done(((bf16[16,256,1024]{2,1,0:T(8,128)(2,1)}), bf16[16,256,1024]{2,1,0:T(8,128)(2,1)}, u32[]{:S(2)}, u32[]{:S(2)}) %all-to-all-start) | async-done | bytes 8388640 | tf_op jit(solution)/shard_map/all_to_all | solution.py:117
  164.3 6.8 %multiply_convert_fusion.20 = (bf16[256,1024]{1,0:T(8,128)(2,1)S(1)}, bf16[256,1024]{1,0:T(8,128)(2,1)}) fusion(f32[256,1024]{1,0:T(8,128)} %copy.101, bf16[4096,1024]{1,0:T(8,128)(2,1)} %bitcast.1, bf16[1,256,4096]{2,1,0:T(8,128)(2,1)S(1)} %copy-done), kind=kOutput, calls=%fused_computation.44 | convolution fusion | flops 2148532224 | bytes 12582912 | tf_op jit(solution)/shard_map/dot_general | solution.py:114
  172.6 17.3 %all-gather = f32[8,1,16,1]{2,3,1,0:T(1,128)S(1)} all-gather(f32[1,1,16,1]{2,3,1,0:T(1,128)S(1)} %get-tuple-element.390), channel_id=2, replica_groups=mesh['seq'=8,'tensor'=8,'dp'=2] {'seq'}, dimensions={0}, use_global_device_ids=true | all-gather | bytes 576 | tf_op jit(solution)/shard_map/all_gather | solution.py:13
  190.9 8.6 %while.19 = (s32[]{:T(128)}, f32[1,16,64,128]{3,2,1,0:T(8,128)S(1)}, s32[]{:T(128)}, f32[8,1,16]{2,1,0:T(1,128)S(1)}, f32[8,1,16,64,128]{4,3,2,1,0:T(8,128)}, /*index=5*/s32[]{:T(128)}, s32[]{:T(128)}) while((s32[]{:T(128)}, f32[1,16,64,128]{3,2,1,0:T(8,128)S(1)}, s32[]{:T(128)}, f32[8,1,16]{2,1,0:T(1,128)S(1)}, ...), condition=%wide.region_6.7_spmd.clone, body=%wide.region_5.6_spmd.clone.sunk | while | flops 524292 | bytes 1573161 | solution.py:25
  190.9 1.3 fusion.61
  192.2 1.2 fusion.61
  193.4 1.2 fusion.61
  194.7 1.2 fusion.61
  195.9 1.2 fusion.61
  197.1 1.2 fusion.61
  198.3 1.2 fusion.61
  199.8 2.5 fusion.21
  202.3 5.6 %convert_bitcast_fusion = bf16[4096,1024]{0,1:T(8,128)(2,1)} fusion(bf16[256,1024]{0,1:T(8,128)(2,1)S(1)} %bitcast.204, bf16[1,256,4096]{2,1,0:T(8,128)(2,1)S(1)} %copy-done), kind=kOutput, calls=%fused_computation.6 | convolution fusion | flops 2151677952 | bytes 11010048 | tf_op jit(solution)/shard_map/ld,lh->dh/dot_general | solution.py:179
  208.0 2.1 copy.93
  210.0 2.2 copy.105
  212.2 1.4 convolution_bitcast_fusion.2
  213.6 2.7 convert_reduce_fusion
  217.1 4.7 %rev.7 = f32[8,1,16,64,128]{4,3,2,1,0:T(8,128)} reverse(f32[8,1,16,64,128]{4,3,2,1,0:T(8,128)} %bitcast.192), dimensions={0} | reverse | bytes 8388608 | tf_op jit(solution)/shard_map/rev | solution.py:15
  221.8 8.5 %while.18 = (s32[]{:T(128)}, f32[1,16,64,128]{3,2,1,0:T(8,128)S(1)}, s32[]{:T(128)}, f32[8,1,16]{2,1,0:T(1,128)S(1)}, f32[8,1,16,64,128]{4,3,2,1,0:T(8,128)}, /*index=5*/s32[]{:T(128)}, s32[]{:T(128)}) while((s32[]{:T(128)}, f32[1,16,64,128]{3,2,1,0:T(8,128)S(1)}, s32[]{:T(128)}, f32[8,1,16]{2,1,0:T(1,128)S(1)}, ...), condition=%wide.region_3.4_spmd.clone, body=%wide.region_2.3_spmd.clone.sunk | while | flops 524292 | bytes 1573161 | solution.py:25
  223.0 1.2 fusion.60
  225.4 1.2 fusion.60
  226.7 1.2 fusion.60
  227.9 1.2 fusion.60
  229.1 1.2 fusion.60
  230.7 3.8 %fusion.20 = bf16[1,256,1,16,64]{1,4,3,2,0:T(8,128)(2,1)} fusion(f32[1,256,1,16,64]{1,4,3,2,0:T(8,128)S(1)} %fusion.10, bf16[256,16,64]{0,2,1:T(8,128)(2,1)} %bitcast.202, f32[256,256]{1,0:T(8,128)} %fusion.40, f32[16,256]{1,0:T(8,128)S(1)} %bitcast_add_fusion.2, pred[256,256]{1,0:T(8,128)(4,1)S(1)} %iota_compare_fusion, ...), kind=kOutput, calls=%fused_computation.29 | convolution fusion | flops 140509184 | bytes 3489856 | tf_op jit(solution)/shard_map/vmap(gkij,igkp->jgkp)/dot_general | solution.py:29
  234.4 2.1 copy.112
  237.7 82.3 %reduce-scatter.2.cloned.1.call-done = bf16[256,1024]{0,1:T(8,128)(2,1)} async-done(((bf16[4096,1024]{0,1:T(8,128)(2,1)}), bf16[256,1024]{0,1:T(8,128)(2,1)}) %reduce-scatter.2.cloned.1.call-update) | async-done | bytes 524304 | tf_op jit(solution)/shard_map/reduce_scatter | solution.py:178
  320.1 2.2 copy.113
  (80 shorter events, 10.9 us)
Async XLA Ops:
  7.2 157.1 %copy-start = (bf16[1,256,4096]{2,1,0:T(8,128)(2,1)S(1)}, bf16[1,256,4096]{2,1,0:T(8,128)(2,1)}, u32[]{:S(2)}) copy-start(bf16[1,256,4096]{2,1,0:T(8,128)(2,1)} %param.20) | copy-start | bytes 6291460
  12.7 8.6 %copy-start.8 = (f32[1,16,256]{2,1,0:T(8,128)S(1)}, f32[1,16,256]{2,1,0:T(8,128)}, u32[]{:S(2)}) copy-start(f32[1,16,256]{2,1,0:T(8,128)} %param.16) | copy-start | bytes 49156
  12.7 8.7 %copy-start.9 = (f32[16]{0:T(128)S(1)}, f32[16]{0:T(128)}, u32[]{:S(2)}) copy-start(f32[16]{0:T(128)} %param.17) | copy-start | bytes 196
  12.7 12.7 %copy-start.6 = (bf16[1,256,128]{2,1,0:T(8,128)(2,1)S(1)}, bf16[1,256,128]{2,1,0:T(8,128)(2,1)}, u32[]{:S(2)}) copy-start(bf16[1,256,128]{2,1,0:T(8,128)(2,1)} %param.14) | copy-start | bytes 196612
  12.7 151.6 %all-to-all-start = ((bf16[16,256,1024]{2,1,0:T(8,128)(2,1)}), bf16[16,256,1024]{2,1,0:T(8,128)(2,1)}, u32[]{:S(2)}, u32[]{:S(2)}) async-start(bf16[16,256,1024]{2,1,0:T(8,128)(2,1)} %stack.2), calls=%async_computation | async-start | bytes 16777216 | tf_op jit(solution)/shard_map/all_to_all | solution.py:117
  21.3 169.6 %all-gather.8.cloned.1.call-start = ((), (), s32[]{:S(2)}) async-start(), calls=%async_computation.4 | async-start | bytes 4718592 | tf_op jit(solution)/shard_map/all_gather | solution.py:13
  24.4 2.1 copy-start.4
  24.5 0.8 copy-start.2
  26.5 190.6 %all-gather.6.cloned.1.call-start = ((), (), s32[]{:S(2)}) async-start(), calls=%async_computation.3 | async-start | bytes 4718592 | tf_op jit(solution)/shard_map/all_gather | solution.py:13
  164.3 7.0 %copy-start.7 = (bf16[1,256,128]{2,1,0:T(8,128)(2,1)S(1)}, bf16[1,256,128]{2,1,0:T(8,128)(2,1)}, u32[]{:S(2)}) copy-start(bf16[1,256,128]{2,1,0:T(8,128)(2,1)} %param.15) | copy-start | bytes 196612
  171.3 1.2 copy-start.1
  172.5 147.6 %reduce-scatter.2.cloned.1.call-start = ((), (), s32[]{:S(2)}) async-start(), calls=%async_computation.2 | async-start | bytes 8912896 | tf_op jit(solution)/shard_map/reduce_scatter | solution.py:178
  190.9 8.9 %copy-start.5 = (bf16[1,256,1024]{1,2,0:T(8,128)(2,1)S(1)}, bf16[1,256,1024]{1,2,0:T(8,128)(2,1)}, u32[]{:S(2)}) copy-start(bf16[1,256,1024]{1,2,0:T(8,128)(2,1)} %copy-done.4) | copy-start | bytes 1572868
  190.9 8.9 %copy-start.10 = (f32[16]{0:T(128)S(1)}, f32[16]{0:T(128)}, u32[]{:S(2)}) copy-start(f32[16]{0:T(128)} %param.18) | copy-start | bytes 196
  230.6 5.9 %copy-start.3 = (bf16[1,256,1024]{1,2,0:T(8,128)(2,1)S(1)}, bf16[1,256,1024]{1,2,0:T(8,128)(2,1)}, u32[]{:S(2)}) copy-start(bf16[1,256,1024]{1,2,0:T(8,128)(2,1)} %copy-done.2) | copy-start | bytes 1572868
Sparse Core Ops, SparseCore 0:
  26.6 95.6 all-gather.7
  172.6 42.2 all-gather.5
  219.2 100.8 reduce-scatter.1
